TPU v7x, 32 devices: a whole 2x2x4 slice. The times are simulated.
32 devices in a mesh: tm: 8 (over y, x, core), space: 4 (over z).
Axes of the slice: x: 2, y: 2, z: 4, core: 2. Of those that a mesh axis runs over, the one named last changes fastest.
Arguments:
- frames: bfloat16 [128, 256, 768], P('tm', 'space'), may hold values from -6 to 6
- gain_time: float32 [768], replicated, may hold values from 0.25 to 1.75
- wq_time: bfloat16 [768, 768], replicated, may hold values from -6 to 6
- wkv_time: bfloat16 [768, 512], replicated, may hold values from -6 to 6
- wo_time: bfloat16 [768, 768], replicated, may hold values from -0.21875 to 0.21875
- gain_space: float32 [768], replicated, may hold values from 0.25 to 1.75
- wq_space: bfloat16 [768, 768], replicated, may hold values from -6 to 6
- wkv_space: bfloat16 [768, 512], replicated, may hold values from -6 to 6
- wo_space: bfloat16 [768, 768], replicated, may hold values from -0.21875 to 0.21875
- gain_mlp: float32 [768], replicated, may hold values from 0.25 to 1.75
- w_in: bfloat16 [768, 3072], replicated, may hold values from -0.21875 to 0.21875
- w_out: bfloat16 [3072, 768], replicated, may hold values from -0.109375 to 0.109375
Outputs:
- encoded: bfloat16 [128, 256, 768], P('tm', 'space')
All inputs are finite; a program needn't handle non-finite values.
Results may differ from a plain program's by a relative error of at most 0.025.
The roundings to bfloat16 on the way count: a program that leaves them out, or rounds other values in their place, can miss the bound.
Values may be sent and summed in bfloat16 or wider, within the bound.
A program may use at most 192 MiB of HBM per device.

v0:
```python
import jax
import jax.numpy as jnp
from jax import lax
from jax.sharding import PartitionSpec as P

HEADS = 12
KV_HEADS = 4
HEAD = 64
WINDOW = 8


def extended(x, sides, width):
    for axis, dim in sides:
        size, length = (lax.axis_size(axis), x.shape[dim])
        up = [(i, (i + 1) % size) for i in range(size - 1)]
        down = [(j, i) for i, j in up]
        last = lax.slice_in_dim(x, length - width, length, axis=dim)
        leading = lax.slice_in_dim(x, 0, width, axis=dim)
        before = lax.ppermute(last, axis, up)
        after = lax.ppermute(leading, axis, down)
        x = jnp.concatenate([before, x, after], axis=dim)
    return x


def layer_norm(x, gain):
    xf = x.astype(jnp.float32)
    mean = jnp.mean(xf, axis=-1, keepdims=True)
    var = jnp.mean((xf - mean) * (xf - mean), axis=-1, keepdims=True)
    return ((xf - mean) * lax.rsqrt(var + 1e-06) * gain).astype(jnp.bfloat16)


def project(a, w):
    flat = a.reshape(-1, a.shape[-1])
    return jnp.dot(flat, w, preferred_element_type=jnp.float32).reshape(
        a.shape[:-1] + (w.shape[1],)
    )


def banded_time(queries, padded, valid):
    group = HEADS // KV_HEADS
    count = queries.shape[0]
    patches = queries.shape[1]
    extent = padded.shape[0]
    q_heads = queries.reshape(count, patches, KV_HEADS, group, HEAD)
    k_heads = padded[..., : KV_HEADS * HEAD].reshape(extent, patches, KV_HEADS, HEAD)
    v_heads = padded[..., KV_HEADS * HEAD :].reshape(extent, patches, KV_HEADS, HEAD)
    scores = jnp.einsum(
        "tpgrd,spgd->pgtrs", q_heads, k_heads, preferred_element_type=jnp.float32
    ) / jnp.sqrt(jnp.float32(HEAD))
    scores = jnp.where(valid[:, None, :], scores, jnp.float32(-1e30))
    top = jnp.max(scores, axis=-1, keepdims=True)
    expo = jnp.exp(scores - top)
    weights = (expo / jnp.sum(expo, axis=-1, keepdims=True)).astype(jnp.bfloat16)
    out = jnp.einsum("pgtrs,spgd->tpgrd", weights, v_heads, preferred_element_type=jnp.float32)
    return out.reshape(count, patches, HEADS * HEAD).astype(jnp.bfloat16)


def attend_space(query, keyvals):
    group = HEADS // KV_HEADS
    patches = query.shape[0]
    count = keyvals.shape[0]
    q_heads = query.reshape(patches, KV_HEADS, group, HEAD)
    k_heads = keyvals[:, : KV_HEADS * HEAD].reshape(count, KV_HEADS, HEAD)
    v_heads = keyvals[:, KV_HEADS * HEAD :].reshape(count, KV_HEADS, HEAD)
    scores = jnp.einsum(
        "pgrd,kgd->grpk", q_heads, k_heads, preferred_element_type=jnp.float32
    ) / jnp.sqrt(jnp.float32(HEAD))
    top = jnp.max(scores, axis=-1, keepdims=True)
    expo = jnp.exp(scores - top)
    weights = (expo / jnp.sum(expo, axis=-1, keepdims=True)).astype(jnp.bfloat16)
    out = jnp.einsum("grpk,kgd->pgrd", weights, v_heads, preferred_element_type=jnp.float32)
    return out.reshape(patches, HEADS * HEAD).astype(jnp.bfloat16)


def body(
    frames,
    gain_time,
    wq_time,
    wkv_time,
    wo_time,
    gain_space,
    wq_space,
    wkv_space,
    wo_space,
    gain_mlp,
    w_in,
    w_out,
):
    count = frames.shape[0]
    normed = layer_norm(frames, gain_time)
    queries = project(normed, wq_time).astype(jnp.bfloat16)
    keyvals = project(normed, wkv_time).astype(jnp.bfloat16)
    padded = extended(keyvals, (("tm", 0),), WINDOW)
    extent = padded.shape[0]
    first = lax.axis_index("tm") * count
    total = count * lax.axis_size("tm")
    query_pos = jnp.arange(count, dtype=jnp.int32)[:, None]
    key_pos = jnp.arange(extent, dtype=jnp.int32)[None, :] - WINDOW
    global_key = first + key_pos
    valid = (jnp.abs(key_pos - query_pos) <= WINDOW) & (global_key >= 0) & (global_key < total)
    attended = banded_time(queries, padded, valid)
    after_time = (frames.astype(jnp.float32) + project(attended, wo_time)).astype(jnp.bfloat16)
    normed = layer_norm(after_time, gain_space)
    queries = project(normed, wq_space).astype(jnp.bfloat16)
    keyvals = project(normed, wkv_space).astype(jnp.bfloat16)
    gathered = lax.all_gather(keyvals, "space", axis=1, tiled=True)
    attended = jax.vmap(attend_space)(queries, gathered)
    after_space = (after_time.astype(jnp.float32) + project(attended, wo_space)).astype(
        jnp.bfloat16
    )
    normed = layer_norm(after_space, gain_mlp)
    hidden = jax.nn.gelu(project(normed, w_in), approximate=True).astype(jnp.bfloat16)
    return (after_space.astype(jnp.float32) + project(hidden, w_out)).astype(jnp.bfloat16)


def solution(mesh):
    in_specs = (P("tm", "space", None), P(), P(), P(), P(), P(), P(), P(), P(), P(), P(), P())
    out_specs = P("tm", "space", None)
    return jax.shard_map(body, mesh=mesh, in_specs=in_specs, out_specs=out_specs, check_vma=False)
```

profile of v0, /device:TPU:0, one launch (start us, length us, event | category | flops | bytes accessed | tf_op | source)
XLA Modules:
  0.0 242.4 jit_solution(12706470925719395757)
XLA Ops:
  8.4 2.0 fusion.35
  13.4 3.2 %collective-permute-start = (bf16[8,64,512]{2,1,0:T(8,128)(2,1)}, bf16[8,64,512]{2,1,0:T(8,128)(2,1)}, u32[]{:S(2)}, u32[]{:S(2)}) collective-permute-start(bf16[8,64,512]{2,1,0:T(8,128)(2,1)} %get-tuple-element.9), channel_id=1, source_target_pairs={{0,4},{4,8},{8,12},{12,16},{16,20},{20,24},{24,28},{1,5},{5,9},{9,... | collective-permute-start | bytes 1572872 | tf_op jit(solution)/shard_map/ppermute | solution.py:19
  17.8 2.7 %convolution_convert_fusion.1 = bf16[16,64,768]{2,1,0:T(8,128)(2,1)} fusion(bf16[768,768]{1,0:T(8,128)(2,1)S(1)} %copy-done.11, bf16[16,64,768]{2,1,0:T(8,128)(2,1)S(1)} %copy-done.2, f32[768]{0:T(1024)S(1)} %copy-done.14, f32[16,64]{1,0:T(8,128)S(1)} %add_rsqrt_fusion.2, f32[16,64]{1,0:T(8,128)S(1)} %broadcast_multiply_fusion.2), kind=kOutput, calls=%fused_computation.69 | convolution fusion | flops 1212678144 | bytes 4336640 | tf_op jit(solution)/shard_map/dot_general | solution.py:34
  20.5 9.0 %reshape.113 = bf16[16,64,4,3,64]{4,3,2,1,0:T(4,128)(2,1)} reshape(bf16[16,64,768]{2,1,0:T(8,128)(2,1)} %convolution_convert_fusion.1) | data formatting | bytes 3145728 | tf_op jit(solution)/shard_map/reshape | solution.py:44
  32.3 1.8 reshape.112
  34.1 3.3 %reshape.114 = bf16[32,64,4,64]{3,2,1,0:T(4,128)(2,1)S(1)} reshape(bf16[32,64,256]{2,1,0:T(8,128)(2,1)} %get-tuple-element.8) | data formatting | bytes 2097152 | tf_op jit(solution)/shard_map/reshape | solution.py:45
  37.4 5.9 %fusion.44 = f32[64,4,16,3,32]{4,2,3,1,0:T(8,128)S(1)} fusion(bf16[16,64,4,3,64]{4,3,2,1,0:T(4,128)(2,1)} %reshape.113, bf16[32,64,4,64,1]{3,2,1,0,4:T(4,128)(2,1)S(1)} %bitcast.75), kind=kOutput, calls=%fused_computation.57 | convolution fusion | flops 50331648 | bytes 4194304 | tf_op jit(solution)/shard_map/tpgrd,spgd->pgtrs/dot_general | solution.py:47
  43.3 4.3 %fusion.101 = (f32[64,4,16,3]{2,3,1,0:T(4,128)S(1)}, f32[64,4,16,3,32]{4,2,3,1,0:T(8,128)S(1)}) fusion(f32[64,4,16,3,32]{4,2,3,1,0:T(8,128)S(1)} %fusion.44, pred[16,32]{1,0:T(8,128)(4,1)S(1)} %fusion.87), kind=kOutput, calls=%fused_computation.105 | output fusion | flops 2359327 | bytes 3195392 | tf_op jit(solution)/shard_map/sub | solution.py:52
  47.6 2.6 %convert_bitcast_fusion = bf16[16,64,4,3,64]{4,0,3,2,1:T(8,128)(2,1)S(1)} fusion(f32[64,4,16,3,32]{4,2,3,1,0:T(8,128)S(1)} %get-tuple-element.12, f32[64,4,16,3]{2,3,1,0:T(4,128)S(1)} %get-tuple-element.11, bf16[32,64,4,64,1]{3,2,1,0,4:T(4,128)(2,1)S(1)} %bitcast.77), kind=kOutput, calls=%fused_computation.59 | convolution fusion | flops 51904512 | bytes 4243456 | tf_op jit(solution)/shard_map/pgtrs,spgd->tpgrd/dot_general | solution.py:54
  50.3 3.8 %copy.23 = bf16[16,64,4,3,64]{4,3,2,1,0:T(4,128)(2,1)} copy(bf16[16,64,4,3,64]{4,0,3,2,1:T(8,128)(2,1)S(1)} %convert_bitcast_fusion) | data formatting | bytes 3145728 | tf_op jit(solution)/shard_map/convert_element_type | solution.py:55
  54.1 8.3 %convert_element_type.80 = bf16[16,64,768]{2,1,0:T(8,128)(2,1)} reshape(bf16[16,64,4,3,64]{4,3,2,1,0:T(4,128)(2,1)} %copy.23) | data formatting | bytes 3145728 | tf_op jit(solution)/shard_map/convert_element_type | solution.py:55
  62.5 2.9 %convert_reduce_fusion.1 = (f32[16,64]{1,0:T(8,128)S(1)}, bf16[16,64,768]{2,1,0:T(8,128)(2,1)S(1)}) fusion(bf16[16,64,768]{2,1,0:T(8,128)(2,1)} %convert_element_type.80, bf16[768,768]{1,0:T(8,128)(2,1)S(1)} %copy-done, bf16[16,64,768]{2,1,0:T(8,128)(2,1)S(1)} %copy-done.3), kind=kOutput, calls=%fused_computation.29 | convolution fusion | flops 1211890688 | bytes 5902336 | tf_op jit(solution)/shard_map/dot_general | solution.py:34
  66.6 2.0 convolution_convert_fusion.2
  68.6 3.3 %convolution_convert_fusion = bf16[16,64,768]{2,1,0:T(8,128)(2,1)S(1)} fusion(bf16[768,768]{1,0:T(8,128)(2,1)} %param.18, bf16[16,64,768]{2,1,0:T(8,128)(2,1)} %copy-done.4, f32[768]{0:T(1024)S(1)} %copy-done.15, f32[16,64]{1,0:T(8,128)S(1)} %add_rsqrt_fusion.1, f32[16,64]{1,0:T(8,128)S(1)} %broadcast_multiply_fusion.1), kind=kOutput, calls=%fused_computation.68 | convolution fusion | flops 1212678144 | bytes 4336640 | tf_op jit(solution)/shard_map/dot_general | solution.py:34
  71.9 5.0 %reshape.117 = bf16[16,64,4,3,64]{4,3,2,1,0:T(4,128)(2,1)} reshape(bf16[16,64,768]{2,1,0:T(8,128)(2,1)S(1)} %convolution_convert_fusion) | data formatting | bytes 3145728 | tf_op jit(solution)/shard_map/vmap()/reshape | solution.py:62
  76.9 76.5 %all-gather.2.cloned.1.call-done = bf16[16,256,512]{2,1,0:T(8,128)(2,1)} async-done(((bf16[16,64,512]{2,1,0:T(8,128)(2,1)}), bf16[16,256,512]{2,1,0:T(8,128)(2,1)}) %all-gather.2.cloned.1.call-update) | async-done | bytes 4194320 | tf_op jit(solution)/shard_map/all_gather | solution.py:106
  153.3 4.6 %fusion.98 = (bf16[16,256,256]{2,1,0:T(8,128)(2,1)}, bf16[16,256,256]{2,1,0:T(8,128)(2,1)}) fusion(bf16[16,256,512]{2,1,0:T(8,128)(2,1)} %all-gather.2.cloned.1.call-done), kind=kLoop, calls=%fused_computation.102 | loop fusion | bytes 8388608 | tf_op jit(solution)/shard_map/vmap()/slice | solution.py:63
  158.0 2.8 %copy.25 = bf16[16,256,256]{1,2,0:T(8,128)(2,1)S(1)} copy(bf16[16,256,256]{2,1,0:T(8,128)(2,1)} %get-tuple-element.5) | data formatting | bytes 4194304 | tf_op jit(solution)/shard_map/vmap()/slice | solution.py:63
  160.8 4.3 %copy.24 = bf16[16,256,256]{1,2,0:T(8,128)(2,1)} copy(bf16[16,256,256]{2,1,0:T(8,128)(2,1)} %get-tuple-element.6) | data formatting | bytes 4194304 | tf_op jit(solution)/shard_map/vmap()/slice | solution.py:64
  165.2 8.5 %fusion.42 = f32[16,4,256,64,3]{2,3,4,1,0:T(8,128)} fusion(bf16[16,256,4,64,1]{1,3,4,2,0:T(8,128)(2,1)S(1)} %bitcast.74, bf16[16,64,4,3,64]{4,3,2,1,0:T(4,128)(2,1)} %reshape.117), kind=kOutput, calls=%fused_computation.55 | convolution fusion | flops 402653184 | bytes 16252928 | tf_op jit(solution)/shard_map/vmap(pgrd,kgd->grpk)/dot_general | solution.py:65
  173.7 12.9 %fusion.102 = f32[16,4,3,64]{3,2,1,0:T(4,128)S(1)} fusion(f32[16,4,256,64,3]{2,3,4,1,0:T(8,128)} %fusion.42), kind=kOutput, calls=%fused_computation.106 | output fusion | flops 12583167 | bytes 12632064 | tf_op jit(solution)/shard_map/vmap()/sub | solution.py:69
  186.6 27.1 %fusion.50 = bf16[16,4,64,3,64]{4,2,3,1,0:T(8,128)(2,1)} fusion(bf16[16,256,4,64,1]{1,3,4,2,0:T(8,128)(2,1)} %bitcast.78, f32[16,4,3,64]{3,2,1,0:T(4,128)S(1)} %fusion.102, f32[16,4,256,64,3]{2,3,4,1,0:T(8,128)} %fusion.42), kind=kOutput, calls=%fused_computation.64 | convolution fusion | flops 419180800 | bytes 16302080 | tf_op jit(solution)/shard_map/vmap(grpk,kgd->pgrd)/dot_general | solution.py:71
  213.8 3.6 %convert_reduce_fusion = (f32[16,64]{1,0:T(8,128)S(1)}, bf16[16,64,768]{2,1,0:T(8,128)(2,1)S(1)}) fusion(bf16[16,64,768]{1,2,0:T(8,128)(2,1)} %bitcast.76, bf16[768,768]{1,0:T(8,128)(2,1)S(1)} %copy-done.10, bf16[16,64,768]{2,1,0:T(8,128)(2,1)S(1)} %copy-done.5), kind=kOutput, calls=%fused_computation.26 | convolution fusion | flops 1211890688 | bytes 5902336 | tf_op jit(solution)/shard_map/dot_general | solution.py:34
  219.1 16.2 %fusion.40 = bf16[16,64,768]{2,1,0:T(8,128)(2,1)} fusion(bf16[16,64,768]{2,1,0:T(8,128)(2,1)} %copy-done.6, bf16[3072,768]{1,0:T(8,128)(2,1)} %param.23, bf16[768,3072]{1,0:T(8,128)(2,1)} %param.22, f32[768]{0:T(1024)S(1)} %copy-done.16, f32[16,64]{1,0:T(8,128)S(1)} %add_rsqrt_fusion, f32[16,64]{1,0:T(8,128)S(1)} %broadcast_multiply_fusion), kind=kOutput, calls=%fused_computation.53 | convolution fusion | flops 9698279424 | bytes 12594176 | tf_op jit(solution)/shard_map/dot_general | solution.py:34
  (55 shorter events, 11.6 us)
Async XLA Ops:
  6.5 55.9 %copy-start = (bf16[768,768]{1,0:T(8,128)(2,1)S(1)}, bf16[768,768]{1,0:T(8,128)(2,1)}, u32[]{:S(2)}) copy-start(bf16[768,768]{1,0:T(8,128)(2,1)} %param.16) | copy-start | bytes 3538948
  6.5 3.9 %copy-start.2 = (bf16[16,64,768]{2,1,0:T(8,128)(2,1)S(1)}, bf16[16,64,768]{2,1,0:T(8,128)(2,1)}, u32[]{:S(2)}) copy-start(bf16[16,64,768]{2,1,0:T(8,128)(2,1)} %param.12) | copy-start | bytes 4718596
  6.5 3.9 %copy-start.14 = (f32[768]{0:T(1024)S(1)}, f32[768]{0:T(1024)}, u32[]{:S(2)}) copy-start(f32[768]{0:T(1024)} %param.13) | copy-start | bytes 9220
  6.5 3.9 %copy-start.12 = (bf16[768,512]{1,0:T(8,128)(2,1)S(1)}, bf16[768,512]{1,0:T(8,128)(2,1)}, u32[]{:S(2)}) copy-start(bf16[768,512]{1,0:T(8,128)(2,1)} %param.15) | copy-start | bytes 2359300
  6.5 146.8 %all-gather.2.cloned.1.call-start = ((), (), s32[]{:S(2)}) async-start(), calls=%async_computation | async-start | bytes 5242880 | tf_op jit(solution)/shard_map/all_gather | solution.py:106
  10.5 7.4 %copy-start.11 = (bf16[768,768]{1,0:T(8,128)(2,1)S(1)}, bf16[768,768]{1,0:T(8,128)(2,1)}, u32[]{:S(2)}) copy-start(bf16[768,768]{1,0:T(8,128)(2,1)} %param.14) | copy-start | bytes 3538948
  11.5 1.0 copy-start.7
  13.4 16.2 %collective-permute-start = (bf16[8,64,512]{2,1,0:T(8,128)(2,1)}, bf16[8,64,512]{2,1,0:T(8,128)(2,1)}, u32[]{:S(2)}, u32[]{:S(2)}) collective-permute-start(bf16[8,64,512]{2,1,0:T(8,128)(2,1)} %get-tuple-element.9), channel_id=1, source_target_pairs={{0,4},{4,8},{8,12},{12,16},{16,20},{20,24},{24,28},{1,5},{5,9},{9,... | collective-permute-start | bytes 1572872 | tf_op jit(solution)/shard_map/ppermute | solution.py:19
  16.5 13.1 %collective-permute-start.1 = (bf16[8,64,512]{2,1,0:T(8,128)(2,1)S(1)}, bf16[8,64,512]{2,1,0:T(8,128)(2,1)}, u32[]{:S(2)}, u32[]{:S(2)}) collective-permute-start(bf16[8,64,512]{2,1,0:T(8,128)(2,1)S(1)} %get-tuple-element.10), channel_id=1, source_target_pairs={{4,0},{8,4},{12,8},{16,12},{20,16},{24,20},{28,24},{5,1},{9,5},{13... | collective-permute-start | bytes 1572872 | tf_op jit(solution)/shard_map/ppermute | solution.py:20
  20.5 9.1 %copy-start.8 = (bf16[16,64,512]{2,1,0:T(8,128)(2,1)S(1)}, bf16[16,64,512]{2,1,0:T(8,128)(2,1)}, u32[]{:S(2)}) copy-start(bf16[16,64,512]{2,1,0:T(8,128)(2,1)} %copy-done.7) | copy-start | bytes 3145732
  43.3 4.3 %copy-start.9 = (bf16[32,64,4,64]{3,2,1,0:T(4,128)(2,1)S(1)}, bf16[32,64,4,64]{3,2,1,0:T(4,128)(2,1)}, u32[]{:S(2)}) copy-start(bf16[32,64,4,64]{3,2,1,0:T(4,128)(2,1)} %reshape.112) | copy-start | bytes 3145732
  54.1 8.4 %copy-start.3 = (bf16[16,64,768]{2,1,0:T(8,128)(2,1)S(1)}, bf16[16,64,768]{2,1,0:T(8,128)(2,1)}, u32[]{:S(2)}) copy-start(bf16[16,64,768]{2,1,0:T(8,128)(2,1)} %param.12) | copy-start | bytes 4718596
  62.4 4.1 %copy-start.13 = (bf16[768,512]{1,0:T(8,128)(2,1)S(1)}, bf16[768,512]{1,0:T(8,128)(2,1)}, u32[]{:S(2)}) copy-start(bf16[768,512]{1,0:T(8,128)(2,1)} %param.19) | copy-start | bytes 2359300
  62.5 4.1 %copy-start.15 = (f32[768]{0:T(1024)S(1)}, f32[768]{0:T(1024)}, u32[]{:S(2)}) copy-start(f32[768]{0:T(1024)} %param.17) | copy-start | bytes 9220
  65.4 1.1 copy-start.4
  186.6 27.2 %copy-start.5 = (bf16[16,64,768]{2,1,0:T(8,128)(2,1)S(1)}, bf16[16,64,768]{2,1,0:T(8,128)(2,1)}, u32[]{:S(2)}) copy-start(bf16[16,64,768]{2,1,0:T(8,128)(2,1)} %copy-done.4) | copy-start | bytes 4718596
  186.6 27.2 %copy-start.10 = (bf16[768,768]{1,0:T(8,128)(2,1)S(1)}, bf16[768,768]{1,0:T(8,128)(2,1)}, u32[]{:S(2)}) copy-start(bf16[768,768]{1,0:T(8,128)(2,1)} %param.20) | copy-start | bytes 3538948
  213.8 5.3 %copy-start.16 = (f32[768]{0:T(1024)S(1)}, f32[768]{0:T(1024)}, u32[]{:S(2)}) copy-start(f32[768]{0:T(1024)} %param.21) | copy-start | bytes 9220
  217.4 1.2 copy-start.6
  219.1 16.2 %copy-start.1 = (bf16[768,768]{1,0:T(8,128)(2,1)S(1)}, bf16[768,768]{1,0:T(8,128)(2,1)}, u32[]{:S(2)}) copy-start(bf16[768,768]{1,0:T(8,128)(2,1)} %param.16) | copy-start | bytes 3538948
Sparse Core Ops, SparseCore 0:
  68.7 84.5 all-gather.1
where the time goes:
time: 246 us; the launch traced here: 242 us
  waiting for transfers between devices  76.5 us (31%)
  matrix products  75.9 us (31%)
  local copies, waits for them, and re-layouts  48 us (20%)
  other arithmetic  23.6 us (10%)
  between operations  13.9 us (6%)
  starting transfers between devices  4.48 us (2%)
    all_gather x1, waiting for transfers between devices, body(): gathered = lax.all_gather(keyvals, 'space', axis=1, tiled=True)  76.5 us
    dot_general x7, matrix products, project(): jnp.dot(flat, w, preferred_element_type=jnp.float32)  31.7 us
    dot_general x1, matrix products, attend_space(): jnp.einsum('grpk,kgd->pgrd', weights, v_heads, preferred_element_type=jnp...  27.1 us
    sub x1, other arithmetic, attend_space(): expo = jnp.exp(scores - top)  12.9 us
    convert_element_type x2, local copies, waits for them, and re-layouts, banded_time(): return out.reshape(count, patches, HEADS * HEAD).astype(jnp.bfloat16)  12.2 us
    reshape x1, local copies, waits for them, and re-layouts, banded_time(): q_heads = queries.reshape(count, patches, KV_HEADS, group, HEAD)  9.03 us
    dot_general x1, matrix products, attend_space(): jnp.einsum('pgrd,kgd->grpk', q_heads, k_heads, preferred_element_type=jnp...  8.54 us
    slice x2, local copies, waits for them, and re-layouts, attend_space(): k_heads = keyvals[:, :KV_HEADS * HEAD].reshape(count, KV_HEADS, HEAD)  7.49 us
  transfers between devices with their start and end apart: 3, of which 1 were waited for; matrix products, arithmetic and copies ran while one was open for 8% of the time, Pallas kernels for 0%

commit v1 on v0

v1 whole, which is shorter than its diff:
```python
import functools

import jax
import jax.numpy as jnp
from jax import lax
from jax.experimental import pallas as pl
from jax.experimental.pallas import tpu as pltpu
from jax.sharding import PartitionSpec as P

HEADS = 12
KV_HEADS = 4
HEAD = 64
WINDOW = 8
GROUP = HEADS // KV_HEADS
PAIRS = KV_HEADS // 2
PAIR = 2 * HEAD
KV_HALF = KV_HEADS * HEAD
PATCH = 16
BF = jnp.bfloat16
F32 = jnp.float32
CHUNKS = 2


def mm(a, b):
    return jnp.dot(a, b, preferred_element_type=F32)


def mm_t(a, b):
    return lax.dot_general(a, b, (((1,), (1,)), ((), ())), preferred_element_type=F32)


def norm(x, gain):
    mean = jnp.mean(x, axis=-1, keepdims=True)
    diff = x - mean
    var = jnp.mean(diff * diff, axis=-1, keepdims=True)
    return (diff * lax.rsqrt(var + 1e-06) * gain).astype(BF)


def softmax(s):
    e = jnp.exp(s - jnp.max(s, axis=-1, keepdims=True))
    return (e * (1.0 / jnp.sum(e, axis=-1, keepdims=True))).astype(BF)


def attend(q_tiles, keyvals, pair, bias):
    rows = q_tiles[0].shape[0]
    q = jnp.concatenate(q_tiles, axis=0)
    k = keyvals[:, pair * PAIR : (pair + 1) * PAIR]
    v = keyvals[:, KV_HALF + pair * PAIR : KV_HALF + (pair + 1) * PAIR]
    low = lax.broadcasted_iota(jnp.int32, k.shape, 1) < HEAD
    zero = jnp.zeros_like(k)
    out = None
    for half in range(2):
        mask = low if half == 0 else jnp.logical_not(low)
        s = mm_t(q, jnp.where(mask, k, zero))
        if bias is not None:
            s = (s.reshape(GROUP, rows, s.shape[1]) + bias[None]).reshape(s.shape)
        o = mm(softmax(s), jnp.where(mask, v, zero))
        out = o if out is None else out + o
    out = out.astype(BF)
    return [out[j * rows : (j + 1) * rows] for j in range(GROUP)]


def qkv_kernel(x_ref, gain_ref, wq_ref, wkv_ref, q_ref, kv_ref):
    normed = norm(x_ref[...].astype(F32), gain_ref[...])
    kv_ref[...] = mm(normed, wkv_ref[...]).astype(BF)
    q_ref[...] = (mm(normed, wq_ref[...]) * (HEAD ** -0.5)).astype(BF)


def time_kernel(
    half, patches, edge_ref, x_ref, q_ref, kv_ref, halo_ref, wo_ref, gain_ref, wq_ref, wkv_ref,
    after_ref, q_out, kv_out, attn, bias_ref,
):
    count = x_ref.shape[0]
    extent = count + 2 * WINDOW
    d = x_ref.shape[2]

    @pl.when(pl.program_id(0) == 0)
    def _():
        shape = bias_ref.shape
        row = lax.broadcasted_iota(jnp.int32, shape, 0)
        col = lax.broadcasted_iota(jnp.int32, shape, 1)
        t, s = row // PATCH, col // PATCH
        ok = (row % PATCH == col % PATCH) & (s >= t) & (s <= t + 2 * WINDOW)
        edge = edge_ref[0]
        if half == 0:
            ok = ok & (s >= edge)
        else:
            ok = ok & (s < edge)
        bias_ref[...] = jnp.where(ok, 0.0, -1e30).astype(F32)

    bias = bias_ref[...]
    rows = count * PATCH
    for g in range(patches // PATCH):
        at = slice(g * PATCH, (g + 1) * PATCH)
        own, halo = kv_ref[:, at, :], halo_ref[:, at, :]
        keys = jnp.concatenate([halo, own] if half == 0 else [own, halo], axis=0)
        keys = keys.reshape(extent * PATCH, keys.shape[2])
        for pair in range(PAIRS):
            tiles = []
            for j in range(GROUP):
                c = (pair * GROUP + j) * PAIR
                tiles.append(q_ref[:, at, c : c + PAIR].reshape(rows, PAIR))
            for j, o in enumerate(attend(tiles, keys, pair, bias)):
                c = (pair * GROUP + j) * PAIR
                attn[:, at, c : c + PAIR] = o.reshape(count, PATCH, PAIR)
    total = count * patches
    y = mm(attn[...].reshape(total, d), wo_ref[...])
    after = (x_ref[...].reshape(total, d).astype(F32) + y).astype(BF)
    after_ref[...] = after.reshape(after_ref.shape)
    normed = norm(after.astype(F32), gain_ref[...])
    kv_out[...] = mm(normed, wkv_ref[...]).astype(BF).reshape(kv_out.shape)
    q_out[...] = (mm(normed, wq_ref[...]) * (HEAD ** -0.5)).astype(BF).reshape(q_out.shape)


def mlp_tail(after, attended, wo_ref, gain_ref, win_ref, wout_ref):
    x = (after.astype(F32) + mm(attended, wo_ref[...])).astype(BF)
    normed = norm(x.astype(F32), gain_ref[...])
    ff = win_ref.shape[1]
    step = ff // 4
    acc = x.astype(F32)
    out = None
    for i in range(0, ff, step):
        hidden = jax.nn.gelu(mm(normed, win_ref[:, i : i + step]), approximate=True).astype(BF)
        y = mm(hidden, wout_ref[i : i + step, :])
        out = y if out is None else out + y
    return (acc + out).astype(BF)


def space_kernel(x_ref, q_ref, kv_ref, wo_ref, gain_ref, win_ref, wout_ref, *rest):
    out_ref, attn = rest[-2:]
    count, patches, d = x_ref.shape
    shards = kv_ref.shape[0]
    for f in range(count):
        keys = kv_ref[:, f].reshape(shards * patches, kv_ref.shape[3])
        for pair in range(PAIRS):
            tiles = []
            for j in range(GROUP):
                c = (pair * GROUP + j) * PAIR
                tiles.append(q_ref[f, :, c : c + PAIR])
            for j, o in enumerate(attend(tiles, keys, pair, None)):
                c = (pair * GROUP + j) * PAIR
                attn[f, :, c : c + PAIR] = o
    total = count * patches
    out = mlp_tail(x_ref[...].reshape(total, d), attn[...].reshape(total, d), wo_ref, gain_ref, win_ref, wout_ref)
    out_ref[...] = out.reshape(out_ref.shape)


def whole(shape):
    return pl.BlockSpec(shape, lambda *_: (0,) * len(shape), pipeline_mode=pl.Buffered(1))


def pair_columns(w):
    d = w.shape[0]
    w = w.reshape(d, PAIRS, 2, GROUP, HEAD).transpose(0, 1, 3, 2, 4)
    return w.reshape(d, HEADS * HEAD)


def pair_rows(w):
    d = w.shape[1]
    w = w.reshape(PAIRS, 2, GROUP, HEAD, d).transpose(0, 2, 1, 3, 4)
    return w.reshape(HEADS * HEAD, d)


def params():
    return pltpu.CompilerParams(vmem_limit_bytes=48 << 20)


def body(
    frames, gain_time, wq_time, wkv_time, wo_time, gain_space, wq_space, wkv_space, wo_space,
    gain_mlp, w_in, w_out,
):
    count, patches, d = frames.shape
    kvw = wkv_time.shape[1]
    ff = w_in.shape[1]
    tokens = count * patches
    gains = [g.reshape(1, d) for g in (gain_time, gain_space, gain_mlp)]
    rows = 256
    q, kv = pl.pallas_call(
        qkv_kernel,
        grid=(tokens // rows,),
        in_specs=[
            pl.BlockSpec((rows, d), lambda i: (i, 0)),
            whole((1, d)), whole((d, d)), whole((d, kvw)),
        ],
        out_specs=[pl.BlockSpec((rows, d), lambda i: (i, 0)), pl.BlockSpec((rows, kvw), lambda i: (i, 0))],
        out_shape=[jax.ShapeDtypeStruct((tokens, d), BF), jax.ShapeDtypeStruct((tokens, kvw), BF)],
        compiler_params=params(),
        name="qkv_time",
    )(frames.reshape(tokens, d), gains[0], pair_columns(wq_time), wkv_time)
    q = q.reshape(count, patches, d)
    kv = kv.reshape(count, patches, kvw)

    size = lax.axis_size("tm")
    up = [(i, (i + 1) % size) for i in range(size - 1)]
    down = [(j, i) for i, j in up]
    before = lax.ppermute(kv[count - WINDOW :], "tm", up)
    behind = lax.ppermute(kv[:WINDOW], "tm", down)
    index = lax.axis_index("tm")
    part = count // CHUNKS
    first = jnp.where(index == 0, WINDOW, 0).astype(jnp.int32).reshape(1)
    last = jnp.where(index == size - 1, count, count + WINDOW).astype(jnp.int32).reshape(1)

    block = 32
    wo_t, wq_s, wo_s = pair_rows(wo_time), pair_columns(wq_space), pair_rows(wo_space)
    stages = []
    for half, (edge, halo) in enumerate(((first, before), (last, behind))):
        stages.append(pl.pallas_call(
            functools.partial(time_kernel, half, block),
            grid=(patches // block,),
            in_specs=[
                pl.BlockSpec(memory_space=pltpu.SMEM),
                pl.BlockSpec((part, block, d), lambda i, h=half: (h, i, 0)),
                pl.BlockSpec((part, block, d), lambda i, h=half: (h, i, 0)),
                pl.BlockSpec((count, block, kvw), lambda i: (0, i, 0)),
                pl.BlockSpec((WINDOW, block, kvw), lambda i: (0, i, 0)),
                whole((d, d)), whole((1, d)), whole((d, d)), whole((d, kvw)),
            ],
            out_specs=[
                pl.BlockSpec((part, block, d), lambda i: (0, i, 0)),
                pl.BlockSpec((part, block, d), lambda i: (0, i, 0)),
                pl.BlockSpec((part, block, kvw), lambda i: (0, i, 0)),
            ],
            out_shape=[
                jax.ShapeDtypeStruct((part, patches, d), BF),
                jax.ShapeDtypeStruct((part, patches, d), BF),
                jax.ShapeDtypeStruct((part, patches, kvw), BF),
            ],
            scratch_shapes=[
                pltpu.VMEM((part, block, d), BF),
                pltpu.VMEM((part * PATCH, (part + 2 * WINDOW) * PATCH), F32),
            ],
            compiler_params=params(),
            cost_estimate=pl.CostEstimate(flops=6 * 10**9, bytes_accessed=8 << 20, transcendentals=2 << 20),
            name="time_block",
        )(edge, frames, q, kv, halo, wo_t, gains[1], wq_s, wkv_space))

    shards = lax.axis_size("space")
    gathered = [lax.all_gather(s[2], "space", axis=0, tiled=False) for s in stages]
    fb = 4
    out = None
    for half in range(CHUNKS):
        after, q_s, _ = stages[half]
        prev = [] if out is None else [out]
        out = pl.pallas_call(
            space_kernel,
            grid=(part // fb,),
            in_specs=[
                pl.BlockSpec((fb, patches, d), lambda i: (i, 0, 0)),
                pl.BlockSpec((fb, patches, d), lambda i: (i, 0, 0)),
                pl.BlockSpec((shards, fb, patches, kvw), lambda i: (0, i, 0, 0)),
                whole((d, d)), whole((1, d)), whole((d, ff)), whole((ff, d)),
            ] + [pl.BlockSpec(memory_space=pl.ANY) for _ in prev],
            out_specs=pl.BlockSpec((fb, patches, d), lambda i, h=half: (i + h * (part // fb), 0, 0)),
            out_shape=jax.ShapeDtypeStruct((count, patches, d), BF),
            scratch_shapes=[pltpu.VMEM((fb, patches, d), BF)],
            input_output_aliases={7: 0} if prev else {},
            compiler_params=params(),
            cost_estimate=pl.CostEstimate(flops=8 * 10**9, bytes_accessed=18 << 20, transcendentals=4 << 20),
            name="space_block",
        )(after, q_s, gathered[half], wo_s, gains[2], w_in, w_out, *prev)
    return out


def solution(mesh):
    in_specs = (P("tm", "space", None),) + (P(),) * 11
    out_specs = P("tm", "space", None)
    return jax.shard_map(body, mesh=mesh, in_specs=in_specs, out_specs=out_specs, check_vma=False)
```

time: 246 us -> 162 us (0.66); the launches traced: 242 us -> 162 us
  matrix products: 75.9 us -> 0 us
  Pallas kernels: 0 us -> 60.2 us
  local copies, waits for them, and re-layouts: 48 us -> 22.3 us
  other arithmetic: 23.6 us -> 0 us
  waiting for transfers between devices: 76.5 us -> 62 us
    dot_general x11 -> x0, matrix products: 75.9 us -> none  [the longest x7 31.7 us: project(): jnp.dot(flat, w, preferred_element_type=jnp.float32)]
    pallas_call x0 -> x5, Pallas kernels: none -> 60.2 us  [the longest x2 35.6 us: body(): pl.pallas_call(space_kernel, grid=(part // fb,), in_specs=[pl.BlockSpec((...]
    all_gather x1 -> x2, waiting for transfers between devices: 76.5 us -> 56.3 us  [body(): lax.all_gather(s[2], 'space', axis=0, tiled=False)]
    sub x3 -> x0, other arithmetic: 17.2 us -> none  [the longest x1 12.9 us: attend_space(): expo = jnp.exp(scores - top)]
    slice x5 -> x1, local copies, waits for them, and re-layouts: 13.9 us -> 1.05 us  [body(): before = lax.ppermute(kv[count - WINDOW:], 'tm', up)]
    reshape x4 -> x7, local copies, waits for them, and re-layouts: 19.2 us -> 6.42 us  [the longest x2 4.21 us: pair_columns(): return w.reshape(d, HEADS * HEAD)]
    convert_element_type x2 -> x0, local copies, waits for them, and re-layouts: 12.2 us -> none  [banded_time(): return out.reshape(count, patches, HEADS * HEAD).astype(jnp.bfloat16)]
    unnamed x34 -> x40, local copies, waits for them, and re-layouts: 2.72 us -> 12.7 us
  transfers between devices with their start and end apart: 3 -> 4, of which waited for: 1 -> 3; matrix products, arithmetic and copies ran while one was open for 8% -> 4% of each run, Pallas kernels for 0% -> 17%
where the time goes in v1:
time: 162 us
  waiting for transfers between devices  62 us (38%)
  Pallas kernels  60.2 us (37%)
  local copies, waits for them, and re-layouts  22.3 us (14%)
  between operations  13.6 us (8%)
  starting transfers between devices  3.89 us (2%)
    all_gather x2, waiting for transfers between devices, body(): lax.all_gather(s[2], 'space', axis=0, tiled=False)  56.3 us
    pallas_call x2, Pallas kernels, body(): pl.pallas_call(space_kernel, grid=(part // fb,), in_specs=[pl.BlockSpec((...  35.6 us
    pallas_call x2, Pallas kernels, body(): pl.pallas_call(functools.partial(time_kernel, half, block), grid=(patches...  21 us
    unnamed x40, local copies, waits for them, and re-layouts  12.7 us
    ppermute x1, waiting for transfers between devices, body(): behind = lax.ppermute(kv[:WINDOW], 'tm', down)  5.69 us
    reshape x2, local copies, waits for them, and re-layouts, pair_columns(): return w.reshape(d, HEADS * HEAD)  4.21 us
    pallas_call x1, Pallas kernels, body(): pl.pallas_call(qkv_kernel, grid=(tokens // rows,), in_specs=[pl.BlockSpec...  3.61 us
  transfers between devices with their start and end apart: 4, of which 3 were waited for; matrix products, arithmetic and copies ran while one was open for 4% of the time, Pallas kernels for 17%

profile of v1, /device:TPU:0, one launch (start us, length us, event | category | flops | bytes accessed | tf_op | source)
XLA Modules:
  0.0 162.0 jit_solution(1764254688877239907)
XLA Ops:
  7.2 1.6 copy.27
  8.8 1.1 copy.28
  9.9 1.7 %copy.29.wq_ref = bf16[768,768]{1,0:T(8,128)(2,1)S(1)} copy(bf16[768,768]{0,1:T(8,128)(2,1)} %bitcast.36) | data formatting | bytes 2359296 | tf_op jit(solution)/shard_map/reshape | solution.py:155
  11.9 3.6 %qkv_time.1 = (bf16[1024,768]{1,0:T(8,128)(2,1)S(1)}, bf16[1024,512]{1,0:T(8,128)(2,1)S(1)}) custom-call(bf16[1024,768]{1,0:T(8,128)(2,1)S(1)} %bitcast.25, f32[1,768]{1,0:T(1,128)S(1)} %reshape.52.gain_ref, bf16[768,768]{1,0:T(8,128)(2,1)S(1)} %copy.29.wq_ref, bf16[768,512]{1,0:T(8,128)(2,1)S(1)} %copy-done.3), custom_call_target="tpu_custom_call" | custom-call | tf_op jit(solution)/shard_map/qkv_time/pallas_call | solution.py:178
  15.5 1.1 fusion
  17.0 1.0 copy-done.1
  17.9 2.4 %collective-permute-start.1 = (bf16[8,64,512]{2,1,0:T(8,128)(2,1)}, bf16[8,64,512]{2,1,0:T(8,128)(2,1)S(1)}, u32[]{:S(2)}, u32[]{:S(2)}) collective-permute-start(bf16[8,64,512]{2,1,0:T(8,128)(2,1)} %bitcast.19), channel_id=1, source_target_pairs={{0,4},{4,8},{8,12},{12,16},{16,20},{20,24},{24,28},{1,5},{5,9},{9,... | collective-permute-start | bytes 1572872 | tf_op jit(solution)/shard_map/ppermute | solution.py:196
  20.5 1.6 copy.31
  22.0 1.1 copy.32
  23.1 2.5 %copy.33.wq_ref = bf16[768,768]{1,0:T(8,128)(2,1)} copy(bf16[768,768]{0,1:T(8,128)(2,1)} %bitcast.37) | data formatting | bytes 2359296 | tf_op jit(solution)/shard_map/reshape | solution.py:155
  25.7 10.5 %time_block.3 = (bf16[8,64,768]{2,1,0:T(8,128)(2,1)S(1)}, bf16[8,64,768]{2,1,0:T(8,128)(2,1)S(1)}, bf16[8,64,512]{2,1,0:T(8,128)(2,1)}) custom-call(s32[1]{0:T(128)} %bitcast.18.edge_ref, bf16[16,64,768]{2,1,0:T(8,128)(2,1)} %x_ref.3, bf16[16,64,768]{2,1,0:T(8,128)(2,1)} %bitcast.34, bf16[16,64,512]{2,1,0:T(8,128)(2,1)S(1)} %bitcast.30, ...), custom_call_target="tpu_custom_call" | custom-call | flops 6000000000 | bytes 8388608 | tf_op jit(solution)/shard_map/time_block/pallas_call | solution.py:207
  36.2 0.9 copy-done.12
  37.1 0.9 copy-done.14
  38.1 1.5 collective-permute-start
  39.5 5.7 %collective-permute-done.halo_ref = bf16[8,64,512]{2,1,0:T(8,128)(2,1)S(1)} collective-permute-done((bf16[8,64,512]{2,1,0:T(8,128)(2,1)}, bf16[8,64,512]{2,1,0:T(8,128)(2,1)S(1)}, u32[]{:S(2)}, u32[]{:S(2)}) %collective-permute-start) | collective-permute-done | bytes 524320 | tf_op jit(solution)/shard_map/ppermute | solution.py:197
  45.2 10.5 %time_block.2 = (bf16[8,64,768]{2,1,0:T(8,128)(2,1)S(1)}, bf16[8,64,768]{2,1,0:T(8,128)(2,1)S(1)}, bf16[8,64,512]{2,1,0:T(8,128)(2,1)}) custom-call(s32[1]{0:T(128)} %bitcast.edge_ref, bf16[16,64,768]{2,1,0:T(8,128)(2,1)} %x_ref.3, bf16[16,64,768]{2,1,0:T(8,128)(2,1)} %bitcast.35, bf16[16,64,512]{2,1,0:T(8,128)(2,1)S(1)} %bitcast.31, ...), custom_call_target="tpu_custom_call" | custom-call | flops 6000000000 | bytes 8388608 | tf_op jit(solution)/shard_map/time_block/pallas_call | solution.py:207
  57.5 1.4 copy.34
  58.9 30.9 %all-gather.7.cloned.1.call-done = bf16[32,64,512]{2,1,0:T(8,128)(2,1)} async-done(((bf16[8,64,512]{2,1,0:T(8,128)(2,1)}), bf16[32,64,512]{2,1,0:T(8,128)(2,1)}) %all-gather.7.cloned.1.call-update) | async-done | bytes 2097168 | tf_op jit(solution)/shard_map/all_gather | solution.py:238
  89.8 1.6 copy-done.4
  91.4 1.1 copy-done.15
  92.5 17.9 %space_block.2.rest_0_ = bf16[16,64,768]{2,1,0:T(8,128)(2,1)} custom-call(bf16[8,64,768]{2,1,0:T(8,128)(2,1)S(1)} %copy-done.13, bf16[8,64,768]{2,1,0:T(8,128)(2,1)S(1)} %copy-done.15, bf16[4,8,64,512]{3,2,1,0:T(8,128)(2,1)S(1)} %bitcast.32, bf16[768,768]{1,0:T(8,128)(2,1)S(1)} %bitcast.28, f32[1,768]{1,0:T(1,128)S(1)} %reshape.64.gain_ref, ...), custom_call_target="tpu_custom_call" | custom-call | flops 8000000000 | bytes 18874368 | tf_op jit(solution)/shard_map/space_block/pallas_call | solution.py:244
  110.4 25.4 %all-gather.5.cloned.1.call-done = bf16[32,64,512]{2,1,0:T(8,128)(2,1)} async-done(((bf16[8,64,512]{2,1,0:T(8,128)(2,1)}), bf16[32,64,512]{2,1,0:T(8,128)(2,1)}) %all-gather.5.cloned.1.call-update) | async-done | bytes 2097168 | tf_op jit(solution)/shard_map/all_gather | solution.py:238
  135.8 1.6 copy-done.5
  137.4 17.8 %space_block.3 = bf16[16,64,768]{2,1,0:T(8,128)(2,1)} custom-call(bf16[8,64,768]{2,1,0:T(8,128)(2,1)S(1)} %copy-done.9, bf16[8,64,768]{2,1,0:T(8,128)(2,1)S(1)} %copy-done.11, bf16[4,8,64,512]{3,2,1,0:T(8,128)(2,1)S(1)} %bitcast.33, bf16[768,768]{1,0:T(8,128)(2,1)S(1)} %bitcast.29, f32[1,768]{1,0:T(1,128)S(1)} %reshape.64.gain_ref, ...), custom_call_target="tpu_custom_call", output_to_operand_aliasing={{}: (7, {})} | custom-call | flops 8000000000 | bytes 18874368 | tf_op jit(solution)/shard_map/space_block/pallas_call | solution.py:244
  (41 shorter events, 3.3 us)
Async XLA Ops:
  6.5 83.3 %all-gather.7.cloned.1.call-start = ((), (), s32[]{:S(2)}) async-start(), calls=%async_computation.1 | async-start | bytes 2621440 | tf_op jit(solution)/shard_map/all_gather | solution.py:238
  9.9 1.8 %copy-start = (bf16[16,64,768]{2,1,0:T(8,128)(2,1)S(1)}, bf16[16,64,768]{2,1,0:T(8,128)(2,1)}, u32[]{:S(2)}) copy-start(bf16[16,64,768]{2,1,0:T(8,128)(2,1)} %x_ref.3) | copy-start | bytes 4718596
  9.9 2.0 %copy-start.3 = (bf16[768,512]{1,0:T(8,128)(2,1)S(1)}, bf16[768,512]{1,0:T(8,128)(2,1)}, u32[]{:S(2)}) copy-start(bf16[768,512]{1,0:T(8,128)(2,1)} %wkv_ref.3) | copy-start | bytes 2359300
  15.5 1.5 copy-start.6
  15.5 4.9 %copy-start.17 = (f32[768]{0:T(1024)S(1)}, f32[768]{0:T(1024)}, u32[]{:S(2)}) copy-start(f32[768]{0:T(1024)} %param.17) | copy-start | bytes 9220
  15.5 4.9 %copy-start.16 = (bf16[768,768]{1,0:T(8,128)(2,1)S(1)}, bf16[768,768]{1,0:T(8,128)(2,1)}, u32[]{:S(2)}) copy-start(bf16[768,768]{1,0:T(8,128)(2,1)} %param.16) | copy-start | bytes 3538948
  17.0 1.0 copy-start.1
  17.9 7.7 %collective-permute-start.1 = (bf16[8,64,512]{2,1,0:T(8,128)(2,1)}, bf16[8,64,512]{2,1,0:T(8,128)(2,1)S(1)}, u32[]{:S(2)}, u32[]{:S(2)}) collective-permute-start(bf16[8,64,512]{2,1,0:T(8,128)(2,1)} %bitcast.19), channel_id=1, source_target_pairs={{0,4},{4,8},{8,12},{12,16},{16,20},{20,24},{24,28},{1,5},{5,9},{9,... | collective-permute-start | bytes 1572872 | tf_op jit(solution)/shard_map/ppermute | solution.py:196
  23.1 2.5 %copy-start.2 = (bf16[1024,512]{1,0:T(8,128)(2,1)S(1)}, bf16[1024,512]{1,0:T(8,128)(2,1)}, u32[]{:S(2)}) copy-start(bf16[1024,512]{1,0:T(8,128)(2,1)} %copy-done.1) | copy-start | bytes 3145732
  23.1 2.5 %copy-start.7 = (bf16[768,512]{1,0:T(8,128)(2,1)S(1)}, bf16[768,512]{1,0:T(8,128)(2,1)}, u32[]{:S(2)}) copy-start(bf16[768,512]{1,0:T(8,128)(2,1)} %wkv_ref.5) | copy-start | bytes 2359300
  36.2 0.9 copy-start.12
  37.1 0.9 copy-start.14
  38.0 97.8 %all-gather.5.cloned.1.call-start = ((), (), s32[]{:S(2)}) async-start(), calls=%async_computation | async-start | bytes 2621440 | tf_op jit(solution)/shard_map/all_gather | solution.py:238
  38.1 7.2 %collective-permute-start = (bf16[8,64,512]{2,1,0:T(8,128)(2,1)}, bf16[8,64,512]{2,1,0:T(8,128)(2,1)S(1)}, u32[]{:S(2)}, u32[]{:S(2)}) collective-permute-start(bf16[8,64,512]{2,1,0:T(8,128)(2,1)} %bitcast.42), channel_id=1, source_target_pairs={{4,0},{8,4},{12,8},{16,12},{20,16},{24,20},{28,24},{5,1},{9,5},{13... | collective-permute-start | bytes 1572872 | tf_op jit(solution)/shard_map/ppermute | solution.py:197
  45.2 12.2 %copy-start.18 = (f32[768]{0:T(1024)S(1)}, f32[768]{0:T(1024)}, u32[]{:S(2)}) copy-start(f32[768]{0:T(1024)} %param.21) | copy-start | bytes 9220
  55.7 0.9 copy-start.8
  56.6 0.9 copy-start.10
  57.5 32.3 %copy-start.13 = (bf16[8,64,768]{2,1,0:T(8,128)(2,1)S(1)}, bf16[8,64,768]{2,1,0:T(8,128)(2,1)}, u32[]{:S(2)}) copy-start(bf16[8,64,768]{2,1,0:T(8,128)(2,1)} %copy-done.12) | copy-start | bytes 2359300
  89.8 1.6 copy-start.4
  91.4 1.1 copy-start.15
  92.5 43.3 %copy-start.9 = (bf16[8,64,768]{2,1,0:T(8,128)(2,1)S(1)}, bf16[8,64,768]{2,1,0:T(8,128)(2,1)}, u32[]{:S(2)}) copy-start(bf16[8,64,768]{2,1,0:T(8,128)(2,1)} %copy-done.8) | copy-start | bytes 2359300
  92.5 43.3 %copy-start.11 = (bf16[8,64,768]{2,1,0:T(8,128)(2,1)S(1)}, bf16[8,64,768]{2,1,0:T(8,128)(2,1)}, u32[]{:S(2)}) copy-start(bf16[8,64,768]{2,1,0:T(8,128)(2,1)} %copy-done.10) | copy-start | bytes 2359300
  135.8 1.6 copy-start.5
Sparse Core Ops, SparseCore 0:
  38.1 51.6 all-gather.6
  91.4 44.4 all-gather.4

commit v2 on v0

v2 whole, which is shorter than its diff:
```python
import functools

import jax
import jax.numpy as jnp
from jax import lax
from jax.experimental import pallas as pl
from jax.experimental.pallas import tpu as pltpu
from jax.sharding import PartitionSpec as P

HEADS = 12
KV_HEADS = 4
HEAD = 64
WINDOW = 8
GROUP = HEADS // KV_HEADS
PAIRS = KV_HEADS // 2
PAIR = 2 * HEAD
KV_HALF = KV_HEADS * HEAD
PATCH = 16
BF = jnp.bfloat16
F32 = jnp.float32
HALVES = 2
BLOCK = 4
MESH = pl.DeviceIdType.MESH


def mm(a, b):
    return jnp.dot(a, b, preferred_element_type=F32)


def mm_t(a, b):
    return lax.dot_general(a, b, (((1,), (1,)), ((), ())), preferred_element_type=F32)


def norm(x, gain):
    mean = jnp.mean(x, axis=-1, keepdims=True)
    diff = x - mean
    var = jnp.mean(diff * diff, axis=-1, keepdims=True)
    return (diff * lax.rsqrt(var + 1e-06) * gain).astype(BF)


def softmax(s):
    e = jnp.exp(s - jnp.max(s, axis=-1, keepdims=True))
    return (e * (1.0 / jnp.sum(e, axis=-1, keepdims=True))).astype(BF)


def attend(q_tiles, keyvals, pair, bias):
    rows = q_tiles[0].shape[0]
    q = jnp.concatenate(q_tiles, axis=0)
    k = keyvals[:, pair * PAIR : (pair + 1) * PAIR]
    v = keyvals[:, KV_HALF + pair * PAIR : KV_HALF + (pair + 1) * PAIR]
    low = lax.broadcasted_iota(jnp.int32, k.shape, 1) < HEAD
    zero = jnp.zeros_like(k)
    out = None
    for half in range(2):
        mask = low if half == 0 else jnp.logical_not(low)
        s = mm_t(q, jnp.where(mask, k, zero))
        if bias is not None:
            s = (s.reshape(GROUP, rows, s.shape[1]) + bias[None]).reshape(s.shape)
        o = mm(softmax(s), jnp.where(mask, v, zero))
        out = o if out is None else out + o
    out = out.astype(BF)
    return [out[j * rows : (j + 1) * rows] for j in range(GROUP)]


def gelu_mlp(normed, win_ref, wout_ref):
    ff = win_ref.shape[1]
    step = ff // 4
    out = None
    for i in range(0, ff, step):
        hidden = jax.nn.gelu(mm(normed, win_ref[:, i : i + step]), approximate=True).astype(BF)
        y = mm(hidden, wout_ref[i : i + step, :])
        out = y if out is None else out + y
    return out


def pair_order():
    return [(p * 2 + b) * GROUP + j for p in range(PAIRS) for j in range(GROUP) for b in range(2)]


def pair_columns(src, dst):
    order = pair_order()
    for i in range(0, HEADS, 2):
        halves = [src[:, h * HEAD : (h + 1) * HEAD] for h in order[i : i + 2]]
        dst[:, i * HEAD : (i + 2) * HEAD] = jnp.concatenate(halves, axis=1)


def kernel(
    shards,
    x_hbm, gt_ref, wqt_hbm, wkvt_hbm, wot_hbm, gs_ref, wqs_hbm, wkvs_hbm, wos_hbm, gm_ref, win_hbm, wout_hbm,
    out_hbm,
    x, raw, wqt, wkvt, wot, wqs, wkvs, wos, win, wout,
    q, kv, before, behind, attn, after, gathered, bias_ref, outs,
    in_sem, row_sem, out_sem, halo_send, halo_recv, right_send, left_send, left_recv, right_recv,
):
    count, patches, d = x.shape
    tm, size = lax.axis_index("tm"), lax.axis_size("tm")
    me = lax.axis_index("space")
    groups = patches // PATCH
    part = count // HALVES
    blocks = count // BLOCK
    extent = part + 2 * WINDOW
    nxt, prv = lax.rem(tm + 1, size), lax.rem(tm + size - 1, size)

    loads = [
        pltpu.make_async_copy(s, t, in_sem.at[i])
        for i, (s, t) in enumerate((
            (x_hbm, x), (wkvt_hbm, wkvt), (wqt_hbm, raw.at[0]), (wqs_hbm, raw.at[1]),
            (wkvs_hbm, wkvs), (win_hbm, win), (wout_hbm, wout),
        ))
    ]
    order = pair_order()

    def rows_in(src, dst, n):
        return [
            pltpu.make_async_copy(
                src.at[h * HEAD : (h + 1) * HEAD], dst.at[i * HEAD : (i + 1) * HEAD], row_sem.at[n, i]
            )
            for i, h in enumerate(order)
        ]

    wo_loads = [rows_in(wot_hbm, wot, 0), rows_in(wos_hbm, wos, 1)]
    for c in loads[:4]:
        c.start()
    for c in wo_loads[0]:
        c.start()
    for c in loads[4:5]:
        c.start()

    barrier = pltpu.get_barrier_semaphore()
    for other in (nxt, prv):
        pl.semaphore_signal(barrier, inc=1, device_id={"tm": other}, device_id_type=MESH)

    @pl.when(me > 0)
    def _():
        pl.semaphore_signal(barrier, inc=1, device_id={"space": me - 1}, device_id_type=MESH)

    @pl.when(me < shards - 1)
    def _():
        pl.semaphore_signal(barrier, inc=1, device_id={"space": me + 1}, device_id_type=MESH)

    loads[0].wait()
    loads[1].wait()
    chunk = BLOCK

    def kv_step(i, _):
        at = pl.ds(i * chunk, chunk)
        normed = norm(x[at].reshape(chunk * patches, d).astype(F32), gt_ref[...])
        attn[at] = normed.reshape(chunk, patches, d)
        kv[at] = mm(normed, wkvt[...]).astype(BF).reshape(chunk, patches, kv.shape[2])
        return 0

    lax.fori_loop(0, count // chunk, kv_step, 0)

    inner = (me > 0) & (me < shards - 1)

    @pl.when(inner)
    def _():
        pl.semaphore_wait(barrier, 4)

    @pl.when(jnp.logical_not(inner))
    def _():
        pl.semaphore_wait(barrier, 3)

    def halo_copy(side, g):
        at = slice(g * PATCH, (g + 1) * PATCH)
        src = kv.at[count - WINDOW :, at] if side == 0 else kv.at[:WINDOW, at]
        dst = before.at[:, at] if side == 0 else behind.at[:, at]
        return pltpu.make_async_remote_copy(
            src_ref=src, dst_ref=dst, send_sem=halo_send.at[side, g], recv_sem=halo_recv.at[side, g],
            device_id={"tm": nxt if side == 0 else prv}, device_id_type=MESH,
        )

    halos = [[halo_copy(side, g) for g in range(groups)] for side in range(2)]
    for side in range(2):
        for c in halos[side]:
            c.start()

    loads[2].wait()
    pair_columns(raw.at[0], wqt)

    def q_step(i, _):
        at = pl.ds(i * chunk, chunk)
        y = mm(attn[at].reshape(chunk * patches, d), wqt[...]) * (HEAD ** -0.5)
        q[at] = y.astype(BF).reshape(chunk, patches, d)
        return 0

    lax.fori_loop(0, count // chunk, q_step, 0)
    loads[3].wait()
    pair_columns(raw.at[1], wqs)
    for c in wo_loads[1] + loads[5:]:
        c.start()

    def piece(shard, b):
        return gathered.at[shard, b * BLOCK : (b + 1) * BLOCK]

    def to_right(b, dist):
        return pltpu.make_async_remote_copy(
            src_ref=piece(me - dist, b), dst_ref=piece(me - dist, b),
            send_sem=right_send.at[b, dist], recv_sem=left_recv.at[b, dist],
            device_id={"space": me + 1}, device_id_type=MESH,
        )

    def to_left(b, dist):
        return pltpu.make_async_remote_copy(
            src_ref=piece(me + dist, b), dst_ref=piece(me + dist, b),
            send_sem=left_send.at[b, dist], recv_sem=right_recv.at[b, dist],
            device_id={"space": me - 1}, device_id_type=MESH,
        )

    def send_right(b, dist):
        @pl.when((me - dist >= 0) & (me + 1 < shards))
        def _():
            to_right(b, dist).start()

    def send_left(b, dist):
        @pl.when((me + dist < shards) & (me > 0))
        def _():
            to_left(b, dist).start()

    def forward(b, dist):
        @pl.when(me - dist >= 0)
        def _():
            pltpu.make_async_remote_copy(
                src_ref=piece(me - dist, b), dst_ref=piece(me - dist, b),
                send_sem=right_send.at[b, dist - 1], recv_sem=left_recv.at[b, dist - 1],
                device_id={"space": me - 1}, device_id_type=MESH,
            ).wait_recv()

        if dist < shards - 1:
            send_right(b, dist)

        @pl.when(me + dist < shards)
        def _():
            pltpu.make_async_remote_copy(
                src_ref=piece(me + dist, b), dst_ref=piece(me + dist, b),
                send_sem=left_send.at[b, dist - 1], recv_sem=right_recv.at[b, dist - 1],
                device_id={"space": me + 1}, device_id_type=MESH,
            ).wait_recv()

        if dist < shards - 1:
            send_left(b, dist)

    pending = [(b, dist) for b0 in range(0, blocks, 2) for dist in range(1, shards) for b in (b0, b0 + 1)]
    done = []

    def advance(n=1, until=None):
        while pending and (n > 0 or (until is not None and pending_has(until))):
            b, dist = pending.pop(0)
            forward(b, dist)
            done.append((b, dist))
            n -= 1

    def pending_has(b):
        return any(e[0] == b for e in pending)

    row_t = lax.broadcasted_iota(jnp.int32, bias_ref.shape, 0)
    col_t = lax.broadcasted_iota(jnp.int32, bias_ref.shape, 1)
    for half in range(HALVES):
        first = half * part
        rt, cs = row_t // PATCH, col_t // PATCH
        ok = (row_t % PATCH == col_t % PATCH) & (cs >= rt) & (cs <= rt + 2 * WINDOW)
        if half == 0:
            ok = ok & (cs >= jnp.where(tm == 0, WINDOW, 0))
        else:
            ok = ok & (cs < jnp.where(tm == size - 1, count, count + WINDOW))
        bias_ref[...] = jnp.where(ok, 0.0, -1e30).astype(F32)
        halo_ref = before if half == 0 else behind

        for g in range(groups):
            halos[half][g].wait_recv()

        def group_step(g, _):
            at = pl.ds(pl.multiple_of(g * PATCH, PATCH), PATCH)
            own, halo = kv[:, at, :], halo_ref[:, at, :]
            keys = jnp.concatenate([halo, own] if half == 0 else [own, halo], axis=0)
            keys = keys.reshape(extent * PATCH, keys.shape[2])
            bias = bias_ref[...]
            for pair in range(PAIRS):
                tiles = []
                for j in range(GROUP):
                    c = (pair * GROUP + j) * PAIR
                    tiles.append(q[first : first + part, at, c : c + PAIR].reshape(part * PATCH, PAIR))
                for j, o in enumerate(attend(tiles, keys, pair, bias)):
                    c = (pair * GROUP + j) * PAIR
                    attn[first : first + part, at, c : c + PAIR] = o.reshape(part, PATCH, PAIR)
            return 0

        if half == 0:
            lax.fori_loop(0, groups, group_step, 0)
            for c in wo_loads[0]:
                c.wait()
            loads[4].wait()
        else:
            lax.fori_loop(0, groups // 2, group_step, 0)
            advance(1)
            lax.fori_loop(groups // 2, groups, group_step, 0)
            advance(1)

        for b in range(first // BLOCK, (first + part) // BLOCK):
            at = slice(b * BLOCK, (b + 1) * BLOCK)
            y = mm(attn[at].reshape(BLOCK * patches, d), wot[...])
            res = (x[at].reshape(BLOCK * patches, d).astype(F32) + y).astype(BF)
            after[at] = res.reshape(BLOCK, patches, d)
            normed = norm(res.astype(F32), gs_ref[...])
            keyvals = mm(normed, wkvs[...]).astype(BF)
            gathered[me, at] = keyvals.reshape(BLOCK, patches, keyvals.shape[1])
            send_right(b, 0)
            send_left(b, 0)
            y = mm(normed, wqs[...]) * (HEAD ** -0.5)
            q[at] = y.astype(BF).reshape(BLOCK, patches, d)

    for c in wo_loads[1] + loads[5:]:
        c.wait()
    writes = []
    for b in range(blocks):
        advance(0, until=b)
        at = slice(b * BLOCK, (b + 1) * BLOCK)

        def frame_step(i, _):
            f = b * BLOCK + i
            keys = gathered[:, f].reshape(shards * patches, gathered.shape[3])
            for pair in range(PAIRS):
                tiles = []
                for j in range(GROUP):
                    c = (pair * GROUP + j) * PAIR
                    tiles.append(q[f, :, c : c + PAIR])
                for j, o in enumerate(attend(tiles, keys, pair, None)):
                    c = (pair * GROUP + j) * PAIR
                    attn[f, :, c : c + PAIR] = o
            return 0

        lax.fori_loop(0, BLOCK // 2, frame_step, 0)
        advance(1)
        lax.fori_loop(BLOCK // 2, BLOCK, frame_step, 0)
        advance(1)
        y = mm(attn[at].reshape(BLOCK * patches, d), wos[...])
        res = (after[at].reshape(BLOCK * patches, d).astype(F32) + y).astype(BF)
        normed = norm(res.astype(F32), gm_ref[...])
        y = (res.astype(F32) + gelu_mlp(normed, win, wout)).astype(BF)
        outs[at] = y.reshape(BLOCK, patches, d)
        write = pltpu.make_async_copy(outs.at[at], out_hbm.at[at], out_sem.at[b])
        write.start()
        writes.append(write)
        advance(1)

    for c in writes:
        c.wait()
    for side in range(2):
        for c in halos[side]:
            c.wait_send()
    for b in range(blocks):
        for dist in range(shards - 1):
            @pl.when((me - dist >= 0) & (me + 1 < shards))
            def _():
                to_right(b, dist).wait_send()

            @pl.when((me + dist < shards) & (me > 0))
            def _():
                to_left(b, dist).wait_send()


def body(*args):
    frames, gain_time, wq_time, wkv_time, wo_time, gain_space, wq_space, wkv_space, wo_space, gain_mlp, w_in, w_out = args
    count, patches, d = frames.shape
    kvw = wkv_time.shape[1]
    ff = w_in.shape[1]
    shards = lax.axis_size("space")
    gains = [g.reshape(1, d) for g in (gain_time, gain_space, gain_mlp)]
    part = count // HALVES
    blocks = count // BLOCK
    groups = patches // PATCH
    hbm = pl.BlockSpec(memory_space=pl.ANY)
    vmem = pl.BlockSpec(memory_space=pltpu.VMEM)
    dma = pltpu.SemaphoreType.DMA
    return pl.pallas_call(
        functools.partial(kernel, shards),
        in_specs=[hbm, vmem, hbm, hbm, hbm, vmem, hbm, hbm, hbm, vmem, hbm, hbm],
        out_specs=hbm,
        out_shape=jax.ShapeDtypeStruct(frames.shape, BF),
        scratch_shapes=[
            pltpu.VMEM((count, patches, d), BF),
            pltpu.VMEM((2, d, d), BF),
            pltpu.VMEM((d, d), BF),
            pltpu.VMEM((d, kvw), BF),
            pltpu.VMEM((d, d), BF),
            pltpu.VMEM((d, d), BF),
            pltpu.VMEM((d, kvw), BF),
            pltpu.VMEM((d, d), BF),
            pltpu.VMEM((d, ff), BF),
            pltpu.VMEM((ff, d), BF),
            pltpu.VMEM((count, patches, d), BF),
            pltpu.VMEM((count, patches, kvw), BF),
            pltpu.VMEM((WINDOW, patches, kvw), BF),
            pltpu.VMEM((WINDOW, patches, kvw), BF),
            pltpu.VMEM((count, patches, d), BF),
            pltpu.VMEM((count, patches, d), BF),
            pltpu.VMEM((shards, count, patches, kvw), BF),
            pltpu.VMEM((part * PATCH, (part + 2 * WINDOW) * PATCH), F32),
            pltpu.VMEM((count, patches, d), BF),
            dma((7,)),
            dma((2, HEADS)),
            dma((blocks,)),
            dma((2, groups)),
            dma((2, groups)),
            dma((blocks, shards)),
            dma((blocks, shards)),
            dma((blocks, shards)),
            dma((blocks, shards)),
        ],
        compiler_params=pltpu.CompilerParams(
            vmem_limit_bytes=60 << 20, collective_id=0, has_side_effects=True
        ),
        name="encoder_block",
    )(frames, gains[0], wq_time, wkv_time, wo_time, gains[1], wq_space, wkv_space, wo_space, gains[2], w_in, w_out)


def solution(mesh):
    in_specs = (P("tm", "space", None),) + (P(),) * 11
    out_specs = P("tm", "space", None)
    return jax.shard_map(body, mesh=mesh, in_specs=in_specs, out_specs=out_specs, check_vma=False)
```

time: 246 us -> 112 us (0.46); the launches traced: 242 us -> 111 us
  Pallas kernels: 0 us -> 105 us
  waiting for transfers between devices: 76.5 us -> 0 us
  matrix products: 75.9 us -> 0 us
  local copies, waits for them, and re-layouts: 48 us -> 6.49 us
  other arithmetic: 23.6 us -> 0 us
  between operations: 13.9 us -> 0.01 us
  starting transfers between devices: 4.48 us -> 0 us
    pallas_call x0 -> x1, Pallas kernels: none -> 105 us  [body(): pl.pallas_call(functools.partial(kernel, shards), in_specs=[hbm, vmem, hb...]
    all_gather x1 -> x0, waiting for transfers between devices: 76.5 us -> none  [body(): gathered = lax.all_gather(keyvals, 'space', axis=1, tiled=True)]
    dot_general x11 -> x0, matrix products: 75.9 us -> none  [the longest x7 31.7 us: project(): jnp.dot(flat, w, preferred_element_type=jnp.float32)]
    sub x3 -> x0, other arithmetic: 17.2 us -> none  [the longest x1 12.9 us: attend_space(): expo = jnp.exp(scores - top)]
    reshape x4 -> x3, local copies, waits for them, and re-layouts: 19.2 us -> 3.8 us  [body(): gains = [g.reshape(1, d) for g in (gain_time, gain_space, gain_mlp)]]
    slice x5 -> x0, local copies, waits for them, and re-layouts: 13.9 us -> none  [the longest x2 7.49 us: attend_space(): k_heads = keyvals[:, :KV_HEADS * HEAD].reshape(count, KV_HEADS, HEAD)]
    convert_element_type x2 -> x0, local copies, waits for them, and re-layouts: 12.2 us -> none  [banded_time(): return out.reshape(count, patches, HEADS * HEAD).astype(jnp.bfloat16)]
    reduce_sum x4 -> x0, other arithmetic: 4.92 us -> none  [the longest x3 3.09 us: layer_norm(): var = jnp.mean((xf - mean) * (xf - mean), axis=-1, keepdims=True)]
  transfers between devices with their start and end apart: 3 -> 0, of which waited for: 1 -> 0; matrix products, arithmetic and copies ran while one was open for 8% -> 0% of each run, Pallas kernels for 0% -> 0%
where the time goes in v2:
time: 112 us; the launch traced here: 111 us
  Pallas kernels  105 us (94%)
  local copies, waits for them, and re-layouts  6.49 us (6%)
    pallas_call x1, Pallas kernels, body(): pl.pallas_call(functools.partial(kernel, shards), in_specs=[hbm, vmem, hb...  105 us
    reshape x3, local copies, waits for them, and re-layouts, body(): gains = [g.reshape(1, d) for g in (gain_time, gain_space, gain_mlp)]  3.8 us
    unnamed x1, local copies, waits for them, and re-layouts  2.69 us

profile of v2, /device:TPU:0, one launch (start us, length us, event | category | flops | bytes accessed | tf_op | source)
XLA Modules:
  0.0 111.4 jit_solution(15432328928575290433)
XLA Ops:
  0.0 1.3 %reshape.9.gt_ref = f32[1,768]{1,0:T(1,128)} reshape(f32[768]{0:T(1024)} %param.13) | data formatting | bytes 6144 | tf_op jit(solution)/shard_map/reshape | solution.py:368
  1.3 1.3 %reshape.10.gs_ref = f32[1,768]{1,0:T(1,128)} reshape(f32[768]{0:T(1024)} %param.17) | data formatting | bytes 6144 | tf_op jit(solution)/shard_map/reshape | solution.py:368
  2.5 1.3 %reshape.11.gm_ref = f32[1,768]{1,0:T(1,128)} reshape(f32[768]{0:T(1024)} %param.21) | data formatting | bytes 6144 | tf_op jit(solution)/shard_map/reshape | solution.py:368
  3.8 104.9 %encoder_block.1 = bf16[16,64,768]{2,1,0:T(8,128)(2,1)} custom-call(bf16[16,64,768]{2,1,0:T(8,128)(2,1)} %x_hbm.1, f32[1,768]{1,0:T(1,128)} %reshape.9.gt_ref, bf16[768,768]{1,0:T(8,128)(2,1)} %wqt_hbm.1, bf16[768,512]{1,0:T(8,128)(2,1)} %wkvt_hbm.1, bf16[768,768]{1,0:T(8,128)(2,1)} %wot_hbm.1, f32[1,768]{1,0:T(1,128)} %reshape.10.gs_ref, ...), custom_call_target="tpu_custom_call" | custom-call | tf_op jit(solution)/shard_map/encoder_block/pallas_call | solution.py:375
  108.7 2.7 %copy.14 = bf16[16,64,768]{2,1,0:T(8,128)(2,1)} copy(bf16[16,64,768]{2,1,0:T(8,128)(2,1)} %encoder_block.1) | data formatting | bytes 3145728

commit v3 on v2

--- a/solution.py
+++ b/solution.py
@@ -90,7 +90,9 @@
     out_hbm,
     x, raw, wqt, wkvt, wot, wqs, wkvs, wos, win, wout,
     q, kv, before, behind, attn, after, gathered, bias_ref, outs,
+    q_in, host_out, returned,
     in_sem, row_sem, out_sem, halo_send, halo_recv, right_send, left_send, left_recv, right_recv,
+    q_send, q_recv, back_send, back_recv,
 ):
     count, patches, d = x.shape
     tm, size = lax.axis_index("tm"), lax.axis_size("tm")
@@ -99,6 +101,9 @@
     part = count // HALVES
     blocks = count // BLOCK
     extent = part + 2 * WINDOW
+    hosted = blocks // 2 if shards >= 4 else 0
+    is_end = (me == 0) | (me == shards - 1)
+    is_host = (me == 1) | (me == shards - 2)
     nxt, prv = lax.rem(tm + 1, size), lax.rem(tm + size - 1, size)
 
     loads = [
@@ -207,18 +212,43 @@
             device_id={"space": me - 1}, device_id_type=MESH,
         )
 
+    def sends_right(b, dist):
+        return (me - dist >= 0) & (me + (2 if b < hosted else 1) < shards)
+
+    def sends_left(b, dist):
+        return (me + dist < shards) & (me > (1 if b < hosted else 0))
+
+    def query_copy(b, step):
+        at = slice(b * BLOCK, (b + 1) * BLOCK)
+        return pltpu.make_async_remote_copy(
+            src_ref=q.at[at], dst_ref=q_in.at[at], send_sem=q_send.at[b], recv_sem=q_recv.at[b],
+            device_id={"space": me + step}, device_id_type=MESH,
+        )
+
+    def back_copy(b, step):
+        at = slice(b * BLOCK, (b + 1) * BLOCK)
+        return pltpu.make_async_remote_copy(
+            src_ref=host_out.at[at], dst_ref=returned.at[at], send_sem=back_send.at[b], recv_sem=back_recv.at[b],
+            device_id={"space": me + step}, device_id_type=MESH,
+        )
+
+    def on(position, action):
+        @pl.when(me == position)
+        def _():
+            action()
+
     def send_right(b, dist):
-        @pl.when((me - dist >= 0) & (me + 1 < shards))
+        @pl.when(sends_right(b, dist))
         def _():
             to_right(b, dist).start()
 
     def send_left(b, dist):
-        @pl.when((me + dist < shards) & (me > 0))
+        @pl.when(sends_left(b, dist))
         def _():
             to_left(b, dist).start()
 
     def forward(b, dist):
-        @pl.when(me - dist >= 0)
+        @pl.when((me - dist >= 0) & (me < shards - (1 if b < hosted else 0)))
         def _():
             pltpu.make_async_remote_copy(
                 src_ref=piece(me - dist, b), dst_ref=piece(me - dist, b),
@@ -229,7 +259,7 @@
         if dist < shards - 1:
             send_right(b, dist)
 
-        @pl.when(me + dist < shards)
+        @pl.when((me + dist < shards) & (me >= (1 if b < hosted else 0)))
         def _():
             pltpu.make_async_remote_copy(
                 src_ref=piece(me + dist, b), dst_ref=piece(me + dist, b),
@@ -308,6 +338,9 @@
             send_left(b, 0)
             y = mm(normed, wqs[...]) * (HEAD ** -0.5)
             q[at] = y.astype(BF).reshape(BLOCK, patches, d)
+            if b < hosted:
+                on(0, lambda: query_copy(b, 1).start())
+                on(shards - 1, lambda: query_copy(b, -1).start())
 
     for c in wo_loads[1] + loads[5:]:
         c.wait()
@@ -316,23 +349,49 @@
         advance(0, until=b)
         at = slice(b * BLOCK, (b + 1) * BLOCK)
 
-        def frame_step(i, _):
-            f = b * BLOCK + i
-            keys = gathered[:, f].reshape(shards * patches, gathered.shape[3])
-            for pair in range(PAIRS):
-                tiles = []
-                for j in range(GROUP):
-                    c = (pair * GROUP + j) * PAIR
-                    tiles.append(q[f, :, c : c + PAIR])
-                for j, o in enumerate(attend(tiles, keys, pair, None)):
-                    c = (pair * GROUP + j) * PAIR
-                    attn[f, :, c : c + PAIR] = o
-            return 0
-
-        lax.fori_loop(0, BLOCK // 2, frame_step, 0)
-        advance(1)
-        lax.fori_loop(BLOCK // 2, BLOCK, frame_step, 0)
-        advance(1)
+        def attention(source, target, start, stop):
+            def frame_step(i, _):
+                f = b * BLOCK + i
+                keys = gathered[:, f].reshape(shards * patches, gathered.shape[3])
+                for pair in range(PAIRS):
+                    tiles = []
+                    for j in range(GROUP):
+                        c = (pair * GROUP + j) * PAIR
+                        tiles.append(source[f, :, c : c + PAIR])
+                    for j, o in enumerate(attend(tiles, keys, pair, None)):
+                        c = (pair * GROUP + j) * PAIR
+                        target[f, :, c : c + PAIR] = o
+                return 0
+
+            lax.fori_loop(start, stop, frame_step, 0)
+
+        if b < hosted:
+            @pl.when(is_host)
+            def _():
+                query_copy(b, 1).wait_recv()
+                attention(q_in, host_out, 0, BLOCK)
+
+            on(1, lambda: back_copy(b, -1).start())
+            on(shards - 2, lambda: back_copy(b, 1).start())
+            advance(1)
+
+            @pl.when(jnp.logical_not(is_end))
+            def _():
+                attention(q, attn, 0, BLOCK)
+
+            advance(1)
+
+            on(0, lambda: back_copy(b, 1).wait_recv())
+            on(shards - 1, lambda: back_copy(b, -1).wait_recv())
+
+            @pl.when(is_end)
+            def _():
+                attn[at] = returned[at]
+        else:
+            attention(q, attn, 0, BLOCK // 2)
+            advance(1)
+            attention(q, attn, BLOCK // 2, BLOCK)
+            advance(1)
         y = mm(attn[at].reshape(BLOCK * patches, d), wos[...])
         res = (after[at].reshape(BLOCK * patches, d).astype(F32) + y).astype(BF)
         normed = norm(res.astype(F32), gm_ref[...])
@@ -350,13 +409,19 @@
             c.wait_send()
     for b in range(blocks):
         for dist in range(shards - 1):
-            @pl.when((me - dist >= 0) & (me + 1 < shards))
+            @pl.when(sends_right(b, dist))
             def _():
                 to_right(b, dist).wait_send()
 
-            @pl.when((me + dist < shards) & (me > 0))
+            @pl.when(sends_left(b, dist))
             def _():
                 to_left(b, dist).wait_send()
+
+    for b in range(hosted):
+        on(0, lambda: query_copy(b, 1).wait_send())
+        on(shards - 1, lambda: query_copy(b, -1).wait_send())
+        on(1, lambda: back_copy(b, -1).wait_send())
+        on(shards - 2, lambda: back_copy(b, 1).wait_send())
 
 
 def body(*args):
@@ -397,6 +462,9 @@
             pltpu.VMEM((shards, count, patches, kvw), BF),
             pltpu.VMEM((part * PATCH, (part + 2 * WINDOW) * PATCH), F32),
             pltpu.VMEM((count, patches, d), BF),
+            pltpu.VMEM((part, patches, d), BF),
+            pltpu.VMEM((part, patches, d), BF),
+            pltpu.VMEM((part, patches, d), BF),
             dma((7,)),
             dma((2, HEADS)),
             dma((blocks,)),
@@ -406,6 +474,10 @@
             dma((blocks, shards)),
             dma((blocks, shards)),
             dma((blocks, shards)),
+            dma((blocks,)),
+            dma((blocks,)),
+            dma((blocks,)),
+            dma((blocks,)),
         ],
         compiler_params=pltpu.CompilerParams(
             vmem_limit_bytes=60 << 20, collective_id=0, has_side_effects=True

time: 112 us -> 109 us (0.973)
  Pallas kernels: 105 us -> 103 us
    pallas_call x1, Pallas kernels: 105 us -> 103 us  [body(): pl.pallas_call(functools.partial(kernel, shards), in_specs=[hbm, vmem, hb...]
where the time goes in v3:
time: 109 us
  Pallas kernels  103 us (94%)
  local copies, waits for them, and re-layouts  6.49 us (6%)
    pallas_call x1, Pallas kernels, body(): pl.pallas_call(functools.partial(kernel, shards), in_specs=[hbm, vmem, hb...  103 us
    reshape x3, local copies, waits for them, and re-layouts, body(): gains = [g.reshape(1, d) for g in (gain_time, gain_space, gain_mlp)]  3.8 us
    unnamed x1, local copies, waits for them, and re-layouts  2.69 us

profile of v3, /device:TPU:0, one launch (start us, length us, event | category | flops | bytes accessed | tf_op | source)
XLA Modules:
  0.0 109.2 jit_solution(15759433305733673707)
XLA Ops:
  0.0 1.3 %reshape.9.gt_ref = f32[1,768]{1,0:T(1,128)} reshape(f32[768]{0:T(1024)} %param.13) | data formatting | bytes 6144 | tf_op jit(solution)/shard_map/reshape | solution.py:433
  1.3 1.3 %reshape.10.gs_ref = f32[1,768]{1,0:T(1,128)} reshape(f32[768]{0:T(1024)} %param.17) | data formatting | bytes 6144 | tf_op jit(solution)/shard_map/reshape | solution.py:433
  2.5 1.3 %reshape.11.gm_ref = f32[1,768]{1,0:T(1,128)} reshape(f32[768]{0:T(1024)} %param.21) | data formatting | bytes 6144 | tf_op jit(solution)/shard_map/reshape | solution.py:433
  3.8 102.7 %encoder_block.1 = bf16[16,64,768]{2,1,0:T(8,128)(2,1)} custom-call(bf16[16,64,768]{2,1,0:T(8,128)(2,1)} %x_hbm.1, f32[1,768]{1,0:T(1,128)} %reshape.9.gt_ref, bf16[768,768]{1,0:T(8,128)(2,1)} %wqt_hbm.1, bf16[768,512]{1,0:T(8,128)(2,1)} %wkvt_hbm.1, bf16[768,768]{1,0:T(8,128)(2,1)} %wot_hbm.1, f32[1,768]{1,0:T(1,128)} %reshape.10.gs_ref, ...), custom_call_target="tpu_custom_call" | custom-call | tf_op jit(solution)/shard_map/encoder_block/pallas_call | solution.py:440
  106.5 2.7 %copy.14 = bf16[16,64,768]{2,1,0:T(8,128)(2,1)} copy(bf16[16,64,768]{2,1,0:T(8,128)(2,1)} %encoder_block.1) | data formatting | bytes 3145728
